TPU v7x, 32 devices: a whole 2x2x4 slice. The times are simulated.
32 devices in a mesh: groups: 2 (over y), pb: 16 (over z, x, core).
Axes of the slice: x: 2, y: 2, z: 4, core: 2. Of those that a mesh axis runs over, the one named last changes fastest.
Arguments:
- fields: float32 [32, 16, 512], P(('groups', 'pb')), parts along dimension 0, may hold values from -6 to 6
- field_shift: float32 [16, 512], replicated, may hold values from -1 to 1
- cholesky: bfloat16 [512, 1024, 1024], P(None, 'pb'), may hold values from -0.015625 to 0.015625
- onebody: float32 [16, 64], replicated, may hold values from -0.5 to 0.5
- walkers: bfloat16 [32, 1024, 256], P(('groups', 'pb')), parts along dimension 0, may hold values from -6 to 6
Outputs:
- propagated: bfloat16 [32, 1024, 256], P(('groups', 'pb')), parts along dimension 0
There are 2 independent parts, one for each index of `groups`. A program takes and returns all parts, laid end to end along the dimension named above; an argument that names none is the same for every part. Nothing has to cross between parts.
All inputs are finite; a program needn't handle non-finite values.
Results may differ from a plain program's by a relative error of at most 0.0089.
Values may be sent and summed in bfloat16 or wider, within the bound.
A program may use at most 192 MiB of HBM per device.

v0:
```python
import jax
import jax.numpy as jnp
import numpy as np
from jax import lax
from jax.sharding import PartitionSpec as P

TERMS = 6


def per_device(fields, field_shift, cholesky, onebody, walkers):
    devices = lax.axis_size("pb")
    local_walkers = fields.shape[0]
    kpoints = field_shift.shape[0]
    orbitals = onebody.shape[1]
    vectors = field_shift.shape[1]
    rows_here = cholesky.shape[1]
    per_transfer = orbitals // rows_here
    slab = cholesky.reshape(vectors, rows_here * kpoints * orbitals)
    shifted = (fields + field_shift[None]).astype(jnp.bfloat16)
    outgoing = jnp.repeat(shifted, per_transfer, axis=1)
    arrived = lax.all_to_all(outgoing, "pb", split_axis=1, concat_axis=0, tiled=True)
    partial_blocks = jnp.dot(arrived[:, 0, :], slab, preferred_element_type=jnp.float32).astype(
        jnp.bfloat16
    )
    outgoing_blocks = partial_blocks.reshape(devices, local_walkers, rows_here * kpoints * orbitals)
    relayed = lax.all_to_all(outgoing_blocks, "pb", split_axis=0, concat_axis=0, tiled=True)
    relayed = relayed.reshape(kpoints, per_transfer, local_walkers, rows_here, kpoints, orbitals)
    potential = relayed.transpose(2, 4, 1, 3, 0, 5).reshape(
        local_walkers, kpoints, orbitals, kpoints, orbitals
    )
    source_table = (np.arange(kpoints)[:, None] - np.arange(kpoints)[None, :]) % kpoints
    source_index = jnp.asarray(source_table.reshape(1, kpoints, 1, kpoints, 1), dtype=jnp.int32)
    permuted = jnp.take_along_axis(potential, source_index, axis=3)
    permuted = permuted.reshape(local_walkers, kpoints * orbitals, kpoints * orbitals)
    diagonal_term = onebody.reshape(kpoints * orbitals)[None, :, None]
    term = walkers
    total = term.astype(jnp.float32)
    for order in range(1, TERMS):
        product = jnp.einsum("wij,wjc->wic", permuted, term, preferred_element_type=jnp.float32)
        product = product + diagonal_term * term.astype(jnp.float32)
        term = (product * (-1.0 / order)).astype(jnp.bfloat16)
        total = total + term.astype(jnp.float32)
    return total.astype(jnp.bfloat16)


def solution(mesh):
    return jax.shard_map(
        per_device,
        mesh=mesh,
        in_specs=(
            P(("groups", "pb"), None, None),
            P(),
            P(None, "pb", None),
            P(),
            P(("groups", "pb"), None, None),
        ),
        out_specs=P(("groups", "pb"), None, None),
        check_vma=False,
    )
```

profile of v0, /device:TPU:11, one launch (start us, length us, event | category | flops | bytes accessed | tf_op | source)
XLA Modules:
  0.0 204.7 jit_solution(11339887598965163888)
XLA Ops:
  0.0 0.8 fusion.27
  0.8 0.5 broadcast.63
  1.3 0.7 reduce.1
  2.0 0.6 reshape.144
  2.6 6.5 %all-to-all-start = ((bf16[16,2,256]{2,1,0:T(2,128)(2,1)}), bf16[16,2,256]{2,1,0:T(2,128)(2,1)S(1)}, u32[]{:S(2)}, u32[]{:S(2)}) async-start(bf16[16,2,256]{2,1,0:T(2,128)(2,1)} %reshape.144), calls=%async_computation | async-start | bytes 32768 | tf_op jit(solution)/shard_map/all_to_all | solution.py:21
  9.1 58.5 %copy.17 = bf16[64,8,64,1024]{3,1,2,0:T(8,128)(2,1)} copy(bf16[64,8,64,1024]{3,2,1,0:T(8,128)(2,1)} %bitcast.17) | data formatting | bytes 134217728
  67.6 0.0 all-to-all-done
  67.7 22.8 %fusion = bf16[16,1,65536]{2,0,1:T(8,128)(2,1)S(1)} fusion(bf16[512,65536]{1,0:T(8,128)(2,1)} %bitcast.18, bf16[1,16,512]{2,0,1:T(2,128)(2,1)S(1)} %bitcast.91), kind=kOutput, calls=%fused_computation.2 | convolution fusion | flops 1074790400 | bytes 69222400 | tf_op jit(solution)/shard_map/dot_general | solution.py:22
  90.5 2.8 %reduce.2 = bf16[16,65536]{1,0:T(8,128)(2,1)} reduce(bf16[16,1,65536]{2,0,1:T(8,128)(2,1)S(1)} %fusion, bf16[]{:T(256)} %broadcast.63), dimensions={1}, to_apply=%copy.13.reduce_sub_computation | reduce | bytes 4194306 | tf_op jit(solution)/shard_map/reshape | solution.py:25
  93.3 4.0 %reshape.146 = bf16[16,2,32768]{2,1,0:T(2,128)(2,1)} reshape(bf16[16,65536]{1,0:T(8,128)(2,1)} %reduce.2) | data formatting | bytes 4194304
  97.3 0.0 copy-start.1
  97.3 6.1 %all-to-all-start.1 = ((bf16[16,2,32768]{2,1,0:T(2,128)(2,1)}), bf16[16,2,32768]{2,1,0:T(2,128)(2,1)S(1)}, u32[]{:S(2)}, u32[]{:S(2)}) async-start(bf16[16,2,32768]{2,1,0:T(2,128)(2,1)} %reshape.146), calls=%async_computation.1 | async-start | bytes 4194304 | tf_op jit(solution)/shard_map/all_to_all | solution.py:26
  103.5 0.0 copy-done.1
  103.5 0.1 mul.64
  103.5 47.3 %all-to-all-done.1 = bf16[16,2,32768]{2,1,0:T(2,128)(2,1)S(1)} async-done(((bf16[16,2,32768]{2,1,0:T(2,128)(2,1)}), bf16[16,2,32768]{2,1,0:T(2,128)(2,1)S(1)}, u32[]{:S(2)}, u32[]{:S(2)}) %all-to-all-start.1) | async-done | bytes 2097184 | tf_op jit(solution)/shard_map/all_to_all | solution.py:26
  150.9 6.8 %reshape.147 = bf16[16,1,65536]{2,1,0:T(2,128)(2,1)} reshape(bf16[16,2,32768]{2,1,0:T(2,128)(2,1)S(1)} %all-to-all-done.1) | data formatting | bytes 4194304
  157.6 12.4 %reduce = bf16[16,65536]{1,0:T(8,128)(2,1)S(1)} reduce(bf16[16,1,65536]{2,1,0:T(2,128)(2,1)} %reshape.147, bf16[]{:T(256)} %constant.62), dimensions={1}, to_apply=%all_to_all.5.reduce_sub_computation | reduce | bytes 4194306 | tf_op jit(solution)/shard_map/all_to_all | solution.py:26
  170.0 5.8 %reshape.124 = bf16[16,1,1,64,16,64]{5,4,3,0,2,1:T(8,128)(2,1)} reshape(bf16[16,65536]{1,0:T(8,128)(2,1)S(1)} %reduce) | data formatting | bytes 4194304 | tf_op jit(solution)/shard_map/reshape | solution.py:27
  175.8 0.0 copy-start
  175.8 5.3 %copy.30 = bf16[16,1,1,64,16,64]{5,3,0,4,1,2:T(8,128)(2,1)} copy(bf16[16,1,1,64,16,64]{5,4,3,0,2,1:T(8,128)(2,1)} %reshape.124) | data formatting | bytes 4194304 | tf_op jit(solution)/shard_map/reshape | solution.py:27
  181.1 0.0 copy-done
  181.1 5.5 %gather_fusion = bf16[256,64,64]{2,1,0:T(8,128)(2,1)} fusion(bf16[16,64,16,64]{3,1,2,0:T(8,128)(2,1)} %bitcast.88, s32[256]{0:T(256)S(1)} %copy-done), kind=kCustom, calls=%fused_computation | custom fusion | bytes 4196352 | tf_op jit(solution)/shard_map/jit(take_along_axis)/gather | solution.py:33
  186.6 7.6 %copy.29 = bf16[16,16,64,64]{3,1,2,0:T(8,128)(2,1)} copy(bf16[16,16,64,64]{3,2,1,0:T(8,128)(2,1)} %bitcast.89) | data formatting | bytes 4194304 | tf_op jit(solution)/shard_map/jit(take_along_axis)/gather | solution.py:33
  194.3 0.0 copy-start.2
  194.3 5.8 %select_n.42 = bf16[1024,1024]{1,0:T(8,128)(2,1)S(1)} reshape(bf16[16,64,16,64]{3,2,1,0:T(8,128)(2,1)} %bitcast.90) | data formatting | bytes 4194304 | tf_op jit(solution)/shard_map/jit(take_along_axis)/select_n | solution.py:33
  200.0 0.0 copy-done.2
  200.0 0.7 fusion.15
  200.8 0.7 fusion.14
  201.5 0.7 fusion.13
  202.2 0.7 fusion.12
  202.9 1.7 fusion.18
  (1 shorter events, 0.0 us)
Async XLA Ops:
  2.6 65.0 %all-to-all-start = ((bf16[16,2,256]{2,1,0:T(2,128)(2,1)}), bf16[16,2,256]{2,1,0:T(2,128)(2,1)S(1)}, u32[]{:S(2)}, u32[]{:S(2)}) async-start(bf16[16,2,256]{2,1,0:T(2,128)(2,1)} %reshape.144), calls=%async_computation | async-start | bytes 32768 | tf_op jit(solution)/shard_map/all_to_all | solution.py:21
  97.3 6.2 %copy-start.1 = (f32[16,64]{1,0:T(8,128)S(1)}, f32[16,64]{1,0:T(8,128)}, u32[]{:S(2)}) copy-start(f32[16,64]{1,0:T(8,128)} %param.9) | copy-start | bytes 12292
  97.3 53.6 %all-to-all-start.1 = ((bf16[16,2,32768]{2,1,0:T(2,128)(2,1)}), bf16[16,2,32768]{2,1,0:T(2,128)(2,1)S(1)}, u32[]{:S(2)}, u32[]{:S(2)}) async-start(bf16[16,2,32768]{2,1,0:T(2,128)(2,1)} %reshape.146), calls=%async_computation.1 | async-start | bytes 4194304 | tf_op jit(solution)/shard_map/all_to_all | solution.py:26
  175.8 5.3 %copy-start = (s32[256]{0:T(256)S(1)}, s32[256]{0:T(256)}, u32[]{:S(2)}) copy-start(s32[256]{0:T(256)} %constant.61) | copy-start | bytes 3076
  194.3 5.8 %copy-start.2 = (bf16[1,1024,256]{2,1,0:T(8,128)(2,1)S(1)}, bf16[1,1024,256]{2,1,0:T(8,128)(2,1)}, u32[]{:S(2)}) copy-start(bf16[1,1024,256]{2,1,0:T(8,128)(2,1)} %param.10) | copy-start | bytes 1572868
where the time goes:
time: 205 us
  local copies, waits for them, and re-layouts  100 us (49%)
  waiting for transfers between devices  47.3 us (23%)
  matrix products  27.4 us (13%)
  other arithmetic  16.7 us (8%)
  starting transfers between devices  12.7 us (6%)
    unnamed x12, local copies, waits for them, and re-layouts  70.4 us
    all_to_all x1, waiting for transfers between devices, per_device(): lax.all_to_all(outgoing_blocks, 'pb', split_axis=0, concat_axis=0, tiled=...  47.3 us
    dot_general x1, matrix products, per_device(): jnp.dot(arrived[:, 0, :], slab, preferred_element_type=jnp.float32)  22.8 us
    gather x2, local copies, waits for them, and re-layouts, per_device(): permuted = jnp.take_along_axis(potential, source_index, axis=3)  13.2 us
    all_to_all x1, other arithmetic, per_device(): lax.all_to_all(outgoing_blocks, 'pb', split_axis=0, concat_axis=0, tiled=...  12.4 us
    reshape x2, local copies, waits for them, and re-layouts, per_device(): relayed.reshape(kpoints, per_transfer, local_walkers, rows_here, kpoints,...  11.1 us
    all_to_all x1, starting transfers between devices, per_device(): lax.all_to_all(outgoing, 'pb', split_axis=1, concat_axis=0, tiled=True)  6.52 us
    all_to_all x1, starting transfers between devices, per_device(): lax.all_to_all(outgoing_blocks, 'pb', split_axis=0, concat_axis=0, tiled=...  6.15 us
  transfers between devices with their start and end apart: 2, of which 1 were waited for; matrix products, arithmetic and copies ran while one was open for 29% of the time, Pallas kernels for 0%

commit v1 on v0

--- a/solution.py
+++ b/solution.py
@@ -1,13 +1,22 @@
+import functools
+
 import jax
 import jax.numpy as jnp
 import numpy as np
 from jax import lax
+from jax.experimental import pallas as pl
+from jax.experimental.pallas import tpu as pltpu
 from jax.sharding import PartitionSpec as P
 
 TERMS = 6
-
-
-def per_device(fields, field_shift, cholesky, onebody, walkers):
+MESH = pl.DeviceIdType.MESH
+ROWS = 16
+SLOTS = 3
+SPLITS = 2
+PIECE = 2048
+
+
+def plain(fields, field_shift, cholesky, onebody, walkers):
     devices = lax.axis_size("pb")
     local_walkers = fields.shape[0]
     kpoints = field_shift.shape[0]
@@ -43,6 +52,228 @@
     return total.astype(jnp.bfloat16)
 
 
+def kernel(
+    n, nk, norb, fields_ref, shift_ref, chol_ref, onebody_ref, walker_ref, out_ref,
+    fields_in, spread, left, buf, acc, blocks_out, blocks_in, matrix, diag, total, term_a, term_b,
+    fsend, frecv, csem, bsend, brecv,
+):
+    me = lax.axis_index("pb")
+    nchol = chol_ref.shape[0]
+    cols = chol_ref.shape[2] // SPLITS
+    row_blocks = norb // ROWS
+    chunks = row_blocks * SPLITS
+    k_here = cols // norb
+    order = sorted(range(1, n), key=lambda d: abs(2 * d - n))
+    group = 128
+    wide = group * ROWS
+
+    def tensor_copy(c, slot):
+        i, h = c // SPLITS, c % SPLITS
+        return pltpu.make_async_copy(
+            chol_ref.at[:, pl.ds(pl.multiple_of(i * ROWS, ROWS), ROWS), pl.ds(pl.multiple_of(h * cols, cols), cols)],
+            buf.at[slot],
+            csem.at[slot],
+        )
+
+    for c in range(min(SLOTS, chunks)):
+        tensor_copy(c, c).start()
+
+    barrier = pltpu.get_barrier_semaphore()
+    for d in order:
+        pl.semaphore_signal(barrier, inc=1, device_id={"pb": lax.rem(me + d, n)}, device_id_type=MESH)
+    pl.semaphore_wait(barrier, n - 1)
+
+    def field_copy(peer, slot, k):
+        return pltpu.make_async_remote_copy(
+            src_ref=fields_ref.at[peer], dst_ref=fields_in.at[slot], send_sem=fsend.at[k],
+            recv_sem=frecv.at[slot], device_id={"pb": peer}, device_id_type=MESH,
+        )
+
+    for k, d in enumerate(order):
+        field_copy(lax.rem(me + d, n), me, k).start()
+    fields_in[me] = fields_ref[me]
+
+    spread[...] = (
+        lax.broadcasted_iota(jnp.int32, (group, wide), 1) // ROWS
+        == lax.broadcasted_iota(jnp.int32, (group, wide), 0)
+    ).astype(jnp.float32).astype(jnp.bfloat16)
+    square = lax.broadcasted_iota(jnp.int32, (norb, norb), 0) == lax.broadcasted_iota(
+        jnp.int32, (norb, norb), 1
+    )
+    for k in range(nk):
+        row = jnp.broadcast_to(onebody_ref[k : k + 1, :], (norb, norb))
+        column = jnp.sum(jnp.where(square, row, 0.0), axis=1, keepdims=True)
+        diag[k * norb : (k + 1) * norb, :] = jnp.broadcast_to(column, (norb, 128))
+
+    for k, d in enumerate(order):
+        peer = lax.rem(me + n - d, n)
+        field_copy(peer, peer, k).wait_recv()
+
+    shifted = (fields_in[:, 0, :] + shift_ref[pl.ds(me, 1), :]).astype(jnp.bfloat16)
+    mask = (
+        lax.broadcasted_iota(jnp.int32, (ROWS, wide), 1) % ROWS
+        == lax.broadcasted_iota(jnp.int32, (ROWS, wide), 0)
+    )
+    for b in range(nchol // group):
+        spreaded = jnp.dot(
+            shifted[:, b * group : (b + 1) * group], spread[...], preferred_element_type=jnp.float32
+        )
+        for w in range(n):
+            line = jnp.broadcast_to(spreaded[w : w + 1, :], (ROWS, wide))
+            left[w * ROWS : (w + 1) * ROWS, b * wide : (b + 1) * wide] = jnp.where(
+                mask, line, 0.0
+            ).astype(jnp.bfloat16)
+
+    def block_copy(c, peer, slot, k):
+        return pltpu.make_async_remote_copy(
+            src_ref=blocks_out.at[c, peer], dst_ref=blocks_in.at[c, slot], send_sem=bsend.at[c, k],
+            recv_sem=brecv.at[c, slot], device_id={"pb": peer}, device_id_type=MESH,
+        )
+
+    vectors_piece = PIECE // ROWS
+
+    def compute(c, carry):
+        slot = lax.rem(c, SLOTS)
+        tensor_copy(c, slot).wait()
+
+        def piece(p, carry):
+            right = buf[slot, pl.ds(p * vectors_piece, vectors_piece)].reshape(PIECE, cols)
+            part = jnp.dot(
+                left[:, pl.ds(pl.multiple_of(p * PIECE, PIECE), PIECE)], right,
+                preferred_element_type=jnp.float32,
+            )
+
+            @pl.when(p == 0)
+            def _():
+                acc[...] = part
+
+            @pl.when(p > 0)
+            def _():
+                acc[...] += part
+
+            return carry
+
+        lax.fori_loop(0, nchol // vectors_piece, piece, 0)
+
+        @pl.when(c + SLOTS < chunks)
+        def _():
+            tensor_copy(c + SLOTS, slot).start()
+
+        blocks_out[c] = acc[...].astype(jnp.bfloat16).reshape(n, ROWS, cols)
+        for k, d in enumerate(order):
+            block_copy(c, lax.rem(me + d, n), me, k).start()
+        blocks_in[c, me] = blocks_out[c, me]
+        return carry
+
+    lax.fori_loop(0, chunks, compute, 0)
+
+    def assemble(c, carry):
+        i, h = c // SPLITS, c % SPLITS
+        for k, d in enumerate(order):
+            peer = lax.rem(me + n - d, n)
+            block_copy(c, peer, peer, k).wait_recv()
+        for kk in range(k_here):
+            k = h * k_here + kk
+            lane = kk // 2 * 128
+            half = kk % 2 * norb
+            rows = pl.ds(pl.multiple_of(k * norb + i * ROWS, ROWS), ROWS)
+            for pair in range(nk // 2):
+                first = blocks_in[c, lax.rem(k - 2 * pair + nk, nk), :, lane : lane + 128]
+                second = blocks_in[c, lax.rem(k - 2 * pair - 1 + nk, nk), :, lane : lane + 128]
+                matrix[rows, pair * 128 : (pair + 1) * 128] = jnp.concatenate(
+                    [first[:, half : half + norb], second[:, half : half + norb]], axis=1
+                )
+        return carry
+
+    lax.fori_loop(0, chunks, assemble, 0)
+
+    size = nk * norb
+    step = 256
+    for number in range(1, TERMS):
+        source = walker_ref if number == 1 else (term_a if number % 2 == 0 else term_b)
+        target = term_a if number % 2 == 1 else term_b
+        for r in range(0, size, step):
+            rows = slice(r, r + step)
+            product = jnp.dot(matrix[rows, :], source[...], preferred_element_type=jnp.float32)
+            here = source[rows, :].astype(jnp.float32)
+            weight = diag[rows, :]
+            weight = jnp.concatenate([weight] * (here.shape[1] // 128), axis=1)
+            product = product + weight * here
+            term = (product * (-1.0 / number)).astype(jnp.bfloat16)
+            before = here if number == 1 else total[rows, :]
+            after = before + term.astype(jnp.float32)
+            if number < TERMS - 1:
+                target[rows, :] = term
+                total[rows, :] = after
+            else:
+                out_ref[rows, :] = after.astype(jnp.bfloat16)
+
+    for k, d in enumerate(order):
+        field_copy(lax.rem(me + d, n), me, k).wait_send()
+
+    def drain(c, carry):
+        for k, d in enumerate(order):
+            block_copy(c, lax.rem(me + d, n), me, k).wait_send()
+        return carry
+
+    lax.fori_loop(0, chunks, drain, 0)
+
+
+def fused(fields, field_shift, cholesky, onebody, walkers):
+    n = lax.axis_size("pb")
+    nk, norb = onebody.shape
+    nchol = cholesky.shape[0]
+    width = cholesky.shape[2]
+    cols = width // SPLITS
+    chunks = norb // ROWS * SPLITS
+    size, columns = walkers.shape[1:]
+    bf16, f32 = jnp.bfloat16, jnp.float32
+    vmem = pl.BlockSpec(memory_space=pltpu.VMEM)
+    out = pl.pallas_call(
+        functools.partial(kernel, n, nk, norb),
+        out_shape=jax.ShapeDtypeStruct((size, columns), bf16),
+        in_specs=[vmem, vmem, pl.BlockSpec(memory_space=pl.ANY), vmem, vmem],
+        out_specs=vmem,
+        scratch_shapes=[
+            pltpu.VMEM((n, 1, nchol), f32),
+            pltpu.VMEM((128, 128 * ROWS), bf16),
+            pltpu.VMEM((n * ROWS, nchol * ROWS), bf16),
+            pltpu.VMEM((SLOTS, nchol, ROWS, cols), bf16),
+            pltpu.VMEM((n * ROWS, cols), f32),
+            pltpu.VMEM((chunks, n, ROWS, cols), bf16),
+            pltpu.VMEM((chunks, n, ROWS, cols), bf16),
+            pltpu.VMEM((size, size), bf16),
+            pltpu.VMEM((size, 128), f32),
+            pltpu.VMEM((size, columns), f32),
+            pltpu.VMEM((size, columns), bf16),
+            pltpu.VMEM((size, columns), bf16),
+            pltpu.SemaphoreType.DMA((n,)),
+            pltpu.SemaphoreType.DMA((n,)),
+            pltpu.SemaphoreType.DMA((SLOTS,)),
+            pltpu.SemaphoreType.DMA((chunks, n)),
+            pltpu.SemaphoreType.DMA((chunks, n)),
+        ],
+        compiler_params=pltpu.CompilerParams(
+            collective_id=0, has_side_effects=True, vmem_limit_bytes=60 * 1024 * 1024
+        ),
+    )(
+        fields.reshape(nk, 1, nchol), field_shift, cholesky, onebody,
+        walkers.reshape(size, columns),
+    )
+    return out.reshape(walkers.shape)
+
+
+def per_device(fields, field_shift, cholesky, onebody, walkers):
+    n = lax.axis_size("pb")
+    nk, norb = onebody.shape
+    fits = (
+        fields.shape[0] == 1 and n == nk and cholesky.shape[1] == norb and norb == 64
+        and walkers.shape[2] % 128 == 0 and cholesky.shape[0] % 128 == 0
+    )
+    body = fused if fits else plain
+    return body(fields, field_shift, cholesky, onebody, walkers)
+
+
 def solution(mesh):
     return jax.shard_map(
         per_device,

time: 205 us -> 72 us (0.35)
  the two profiles are of different devices: /device:TPU:11 before, /device:TPU:0 now
where the time goes in v1:
time: 72 us; the launch traced here: 71.7 us
  Pallas kernels  68.4 us (95%)
  local copies, waits for them, and re-layouts  3.26 us (5%)
    pallas_call x1, Pallas kernels, fused(): pl.pallas_call(functools.partial(kernel, n, nk, norb), out_shape=jax.Shap...  68.4 us
    unnamed x1, local copies, waits for them, and re-layouts  1.87 us

profile of v1, /device:TPU:0, one launch (start us, length us, event | category | flops | bytes accessed | tf_op | source)
XLA Modules:
  0.0 71.7 jit_solution(2381966993810399741)
XLA Ops:
  0.0 1.4 %reshape.9.fields_ref = f32[16,1,512]{2,1,0:T(1,128)} reshape(f32[1,16,512]{2,1,0:T(8,128)} %param.5) | data formatting | bytes 65536 | tf_op jit(solution)/shard_map/reshape | solution.py:260
  1.4 68.4 %shard_map.55 = bf16[1024,256]{1,0:T(8,128)(2,1)} custom-call(f32[16,1,512]{2,1,0:T(1,128)} %reshape.9.fields_ref, f32[16,512]{1,0:T(8,128)} %shift_ref.1, bf16[512,64,1024]{2,1,0:T(8,128)(2,1)} %chol_ref.1, f32[16,64]{1,0:T(8,128)} %onebody_ref.1, bf16[1024,256]{1,0:T(8,128)(2,1)} %bitcast.3), custom_call_target="tpu_custom_call" | custom-call | tf_op jit(solution)/shard_map/pallas_call | solution.py:232
  69.8 1.9 %copy.7 = bf16[1,1024,256]{2,1,0:T(8,128)(2,1)} copy(bf16[1,1024,256]{2,1,0:T(8,128)(2,1)} %bitcast.2) | data formatting | bytes 1048576

commit v2 on v1

v2 whole, which is shorter than its diff:
```python
import functools

import jax
import jax.numpy as jnp
import numpy as np
from jax import lax
from jax.experimental import pallas as pl
from jax.experimental.pallas import tpu as pltpu
from jax.sharding import PartitionSpec as P

TERMS = 6
MESH = pl.DeviceIdType.MESH
ROWS = 16
SLOTS = 3
SPLITS = 2
PIECE = 2048


def plain(fields, field_shift, cholesky, onebody, walkers):
    devices = lax.axis_size("pb")
    local_walkers = fields.shape[0]
    kpoints = field_shift.shape[0]
    orbitals = onebody.shape[1]
    vectors = field_shift.shape[1]
    rows_here = cholesky.shape[1]
    per_transfer = orbitals // rows_here
    slab = cholesky.reshape(vectors, rows_here * kpoints * orbitals)
    shifted = (fields + field_shift[None]).astype(jnp.bfloat16)
    outgoing = jnp.repeat(shifted, per_transfer, axis=1)
    arrived = lax.all_to_all(outgoing, "pb", split_axis=1, concat_axis=0, tiled=True)
    partial_blocks = jnp.dot(arrived[:, 0, :], slab, preferred_element_type=jnp.float32).astype(
        jnp.bfloat16
    )
    outgoing_blocks = partial_blocks.reshape(devices, local_walkers, rows_here * kpoints * orbitals)
    relayed = lax.all_to_all(outgoing_blocks, "pb", split_axis=0, concat_axis=0, tiled=True)
    relayed = relayed.reshape(kpoints, per_transfer, local_walkers, rows_here, kpoints, orbitals)
    potential = relayed.transpose(2, 4, 1, 3, 0, 5).reshape(
        local_walkers, kpoints, orbitals, kpoints, orbitals
    )
    source_table = (np.arange(kpoints)[:, None] - np.arange(kpoints)[None, :]) % kpoints
    source_index = jnp.asarray(source_table.reshape(1, kpoints, 1, kpoints, 1), dtype=jnp.int32)
    permuted = jnp.take_along_axis(potential, source_index, axis=3)
    permuted = permuted.reshape(local_walkers, kpoints * orbitals, kpoints * orbitals)
    diagonal_term = onebody.reshape(kpoints * orbitals)[None, :, None]
    term = walkers
    total = term.astype(jnp.float32)
    for order in range(1, TERMS):
        product = jnp.einsum("wij,wjc->wic", permuted, term, preferred_element_type=jnp.float32)
        product = product + diagonal_term * term.astype(jnp.float32)
        term = (product * (-1.0 / order)).astype(jnp.bfloat16)
        total = total + term.astype(jnp.float32)
    return total.astype(jnp.bfloat16)


def kernel(
    n, nk, norb, fields_ref, shift_ref, onebody_ref, chol_ref, walker_hbm, out_ref,
    fields_out, fields_in, lines, spread, left, buf, acc, blocks_out, blocks_in, matrix, rows_in, diag,
    total, walker, term_a, term_b, fsend, frecv, csem, bsend, brecv, wsem,
):
    me = lax.axis_index("pb")
    nchol = chol_ref.shape[0]
    cols = chol_ref.shape[2] // SPLITS
    row_blocks = norb // ROWS
    chunks = row_blocks * SPLITS
    k_here = cols // norb
    group = 128
    wide = group * ROWS
    half = n // 2
    mine = me // half
    places = [r for r in range(n) if r != half]

    def peer_of(r):
        side = 1 - mine if r < half else mine
        return side * half + lax.rem(me + r % half, half)

    def tensor_copy(c, slot):
        i, h = c // SPLITS, c % SPLITS
        return pltpu.make_async_copy(
            chol_ref.at[:, pl.ds(pl.multiple_of(i * ROWS, ROWS), ROWS), pl.ds(pl.multiple_of(h * cols, cols), cols)],
            buf.at[slot],
            csem.at[slot],
        )

    barrier = pltpu.get_barrier_semaphore()
    for r in places:
        pl.semaphore_signal(barrier, inc=1, device_id={"pb": peer_of(r)}, device_id_type=MESH)
    for c in range(min(SLOTS, chunks)):
        tensor_copy(c, c).start()
    walker_copy = pltpu.make_async_copy(walker_hbm, walker, wsem)
    walker_copy.start()
    for q in range(nk):
        fields_out[q] = fields_ref[q : q + 1, :]
    fields_in[me] = fields_out[me]
    pl.semaphore_wait(barrier, n - 1)

    def field_copy(peer, slot, r):
        return pltpu.make_async_remote_copy(
            src_ref=fields_out.at[peer], dst_ref=fields_in.at[slot], send_sem=fsend.at[r],
            recv_sem=frecv.at[slot], device_id={"pb": peer}, device_id_type=MESH,
        )

    for r in places:
        field_copy(peer_of(r), me, r).start()

    spread[...] = (
        lax.broadcasted_iota(jnp.int32, (group, wide), 1) // ROWS
        == lax.broadcasted_iota(jnp.int32, (group, wide), 0)
    ).astype(jnp.float32).astype(jnp.bfloat16)
    square = lax.broadcasted_iota(jnp.int32, (norb, norb), 0) == lax.broadcasted_iota(
        jnp.int32, (norb, norb), 1
    )
    for k in range(nk):
        row = jnp.broadcast_to(onebody_ref[k : k + 1, :], (norb, norb))
        column = jnp.sum(jnp.where(square, row, 0.0), axis=1, keepdims=True)
        diag[k * norb : (k + 1) * norb, :] = jnp.broadcast_to(column, (norb, 128))

    for r in places:
        peer = peer_of(r)
        field_copy(peer, peer, r).wait_recv()
    for r in range(n):
        lines[r : r + 1, :] = fields_in[peer_of(r)]

    mask = (
        lax.broadcasted_iota(jnp.int32, (ROWS, wide), 1) % ROWS
        == lax.broadcasted_iota(jnp.int32, (ROWS, wide), 0)
    )
    band = half * ROWS

    def block_copy(c, peer, slot, r):
        return pltpu.make_async_remote_copy(
            src_ref=blocks_out.at[c, r], dst_ref=blocks_in.at[c, slot], send_sem=bsend.at[c, r],
            recv_sem=brecv.at[c, slot], device_id={"pb": peer}, device_id_type=MESH,
        )

    vectors_piece = PIECE // ROWS

    def build(part):
        shifted = (lines[...] + shift_ref[pl.ds(me, 1), :]).astype(jnp.bfloat16)
        for b in range(nchol // group):
            spreaded = jnp.dot(
                shifted[:, b * group : (b + 1) * group], spread[...],
                preferred_element_type=jnp.float32,
            )
            for r in range(part * half, (part + 1) * half):
                line = jnp.broadcast_to(spreaded[r : r + 1, :], (ROWS, wide))
                left[r * ROWS : (r + 1) * ROWS, b * wide : (b + 1) * wide] = jnp.where(
                    mask, line, 0.0
                ).astype(jnp.bfloat16)

    def multiply(c, part):
        slot = lax.rem(c, SLOTS)

        def piece(p, carry):
            right = buf[slot, pl.ds(p * vectors_piece, vectors_piece)].reshape(PIECE, cols)
            product = jnp.dot(
                left[pl.ds(pl.multiple_of(part * band, band), band), pl.ds(pl.multiple_of(p * PIECE, PIECE), PIECE)],
                right, preferred_element_type=jnp.float32,
            )

            @pl.when(p == 0)
            def _():
                acc[...] = product

            @pl.when(p > 0)
            def _():
                acc[...] += product

            return carry

        lax.fori_loop(0, nchol // vectors_piece, piece, 0)
        blocks_out[c, pl.ds(part * half, half)] = acc[...].astype(jnp.bfloat16).reshape(half, ROWS, cols)

    def compute(c, carry):
        slot = lax.rem(c, SLOTS)

        @pl.when(c == 0)
        def _():
            build(0)

        tensor_copy(c, slot).wait()
        for part in range(2):
            if part == 1:

                @pl.when(c == 0)
                def _():
                    build(1)

            multiply(c, part)
            for r in places:
                if r // half == part:
                    block_copy(c, peer_of(r), me, r).start()
        blocks_in[c, me] = blocks_out[c, half]

        @pl.when(c + SLOTS < chunks)
        def _():
            tensor_copy(c + SLOTS, slot).start()

        return carry

    lax.fori_loop(0, chunks, compute, 0)
    walker_copy.wait()

    def finish(product, here, weight, number):
        weight = jnp.concatenate([weight] * (here.shape[1] // 128), axis=1)
        return ((product + weight * here) * (-1.0 / number)).astype(jnp.bfloat16)

    def assemble(c, carry):
        i, h = c // SPLITS, c % SPLITS
        for r in places:
            peer = peer_of(r)
            block_copy(c, peer, peer, r).wait_recv()
        for kk in range(k_here):
            k = h * k_here + kk
            lane = kk // 2 * 128
            off = kk % 2 * norb
            rows = pl.ds(pl.multiple_of(k * norb + i * ROWS, ROWS), ROWS)
            for pair in range(nk // 2):
                first = blocks_in[c, lax.rem(k - 2 * pair + nk, nk), :, lane : lane + 128]
                second = blocks_in[c, lax.rem(k - 2 * pair - 1 + nk, nk), :, lane : lane + 128]
                both = jnp.concatenate([first[:, off : off + norb], second[:, off : off + norb]], axis=1)
                matrix[rows, pair * 128 : (pair + 1) * 128] = both
                rows_in[kk * ROWS : (kk + 1) * ROWS, pair * 128 : (pair + 1) * 128] = both
        product = jnp.dot(rows_in[...], walker[...], preferred_element_type=jnp.float32)
        for kk in range(k_here):
            rows = pl.ds(pl.multiple_of((h * k_here + kk) * norb + i * ROWS, ROWS), ROWS)
            here = walker[rows, :].astype(jnp.float32)
            term = finish(product[kk * ROWS : (kk + 1) * ROWS], here, diag[rows, :], 1)
            term_a[rows, :] = term
            total[rows, :] = here + term.astype(jnp.float32)
        return carry

    lax.fori_loop(0, chunks, assemble, 0)

    size = nk * norb
    step = 256
    for number in range(2, TERMS):
        source, target = (term_a, term_b) if number % 2 == 0 else (term_b, term_a)
        for r in range(0, size, step):
            rows = slice(r, r + step)
            product = jnp.dot(matrix[rows, :], source[...], preferred_element_type=jnp.float32)
            term = finish(product, source[rows, :].astype(jnp.float32), diag[rows, :], number)
            after = total[rows, :] + term.astype(jnp.float32)
            if number < TERMS - 1:
                target[rows, :] = term
                total[rows, :] = after
            else:
                out_ref[rows, :] = after.astype(jnp.bfloat16)

    for r in places:
        field_copy(peer_of(r), me, r).wait_send()

    def drain(c, carry):
        for r in places:
            block_copy(c, peer_of(r), me, r).wait_send()
        return carry

    lax.fori_loop(0, chunks, drain, 0)


def fused(fields, field_shift, cholesky, onebody, walkers):
    n = lax.axis_size("pb")
    nk, norb = onebody.shape
    nchol = cholesky.shape[0]
    width = cholesky.shape[2]
    cols = width // SPLITS
    chunks = norb // ROWS * SPLITS
    size, columns = walkers.shape[1:]
    bf16, f32 = jnp.bfloat16, jnp.float32
    vmem = pl.BlockSpec(memory_space=pltpu.VMEM)
    hbm = pl.BlockSpec(memory_space=pl.ANY)
    out = pl.pallas_call(
        functools.partial(kernel, n, nk, norb),
        out_shape=jax.ShapeDtypeStruct((size, columns), bf16),
        in_specs=[vmem, vmem, vmem, hbm, hbm],
        out_specs=vmem,
        scratch_shapes=[
            pltpu.VMEM((nk, 1, nchol), f32),
            pltpu.VMEM((n, 1, nchol), f32),
            pltpu.VMEM((n, nchol), f32),
            pltpu.VMEM((128, 128 * ROWS), bf16),
            pltpu.VMEM((n * ROWS, nchol * ROWS), bf16),
            pltpu.VMEM((SLOTS, nchol, ROWS, cols), bf16),
            pltpu.VMEM((n // 2 * ROWS, cols), f32),
            pltpu.VMEM((chunks, n, ROWS, cols), bf16),
            pltpu.VMEM((chunks, n, ROWS, cols), bf16),
            pltpu.VMEM((size, size), bf16),
            pltpu.VMEM((cols // norb * ROWS, size), bf16),
            pltpu.VMEM((size, 128), f32),
            pltpu.VMEM((size, columns), f32),
            pltpu.VMEM((size, columns), bf16),
            pltpu.VMEM((size, columns), bf16),
            pltpu.VMEM((size, columns), bf16),
            pltpu.SemaphoreType.DMA((n,)),
            pltpu.SemaphoreType.DMA((n,)),
            pltpu.SemaphoreType.DMA((SLOTS,)),
            pltpu.SemaphoreType.DMA((chunks, n)),
            pltpu.SemaphoreType.DMA((chunks, n)),
            pltpu.SemaphoreType.DMA,
        ],
        compiler_params=pltpu.CompilerParams(
            collective_id=0, has_side_effects=True, vmem_limit_bytes=60 * 1024 * 1024
        ),
    )(
        fields.reshape(nk, nchol), field_shift, onebody, cholesky,
        walkers.reshape(size, columns),
    )
    return out.reshape(walkers.shape)


def per_device(fields, field_shift, cholesky, onebody, walkers):
    n = lax.axis_size("pb")
    nk, norb = onebody.shape
    fits = (
        fields.shape[0] == 1 and n == nk and cholesky.shape[1] == norb and norb == 64
        and walkers.shape[2] % 128 == 0 and cholesky.shape[0] % 128 == 0
    )
    body = fused if fits else plain
    return body(fields, field_shift, cholesky, onebody, walkers)


def solution(mesh):
    return jax.shard_map(
        per_device,
        mesh=mesh,
        in_specs=(
            P(("groups", "pb"), None, None),
            P(),
            P(None, "pb", None),
            P(),
            P(("groups", "pb"), None, None),
        ),
        out_specs=P(("groups", "pb"), None, None),
        check_vma=False,
    )
```

time: 72 us -> 69.1 us (0.960)
  Pallas kernels: 68.4 us -> 67 us
  local copies, waits for them, and re-layouts: 3.26 us -> 1.87 us
    pallas_call x1, Pallas kernels: 68.4 us -> 67 us  [fused(): pl.pallas_call(functools.partial(kernel, n, nk, norb), out_shape=jax.Shap...]
    reshape x1 -> x0, local copies, waits for them, and re-layouts: 1.39 us -> none  [fused(): fields.reshape(nk, 1, nchol)]
where the time goes in v2:
time: 69.1 us; the launch traced here: 68.9 us
  Pallas kernels  67 us (97%)
  local copies, waits for them, and re-layouts  1.87 us (3%)
    pallas_call x1, Pallas kernels, fused(): pl.pallas_call(functools.partial(kernel, n, nk, norb), out_shape=jax.Shap...  67 us
    unnamed x1, local copies, waits for them, and re-layouts  1.87 us

profile of v2, /device:TPU:0, one launch (start us, length us, event | category | flops | bytes accessed | tf_op | source)
XLA Modules:
  0.0 68.9 jit_solution(15161272288414547429)
XLA Ops:
  0.0 67.0 %shard_map.55 = bf16[1024,256]{1,0:T(8,128)(2,1)} custom-call(f32[16,512]{1,0:T(8,128)} %bitcast.5, f32[16,512]{1,0:T(8,128)} %shift_ref.1, f32[16,64]{1,0:T(8,128)} %onebody_ref.1, bf16[512,64,1024]{2,1,0:T(8,128)(2,1)} %chol_ref.1, bf16[1024,256]{1,0:T(8,128)(2,1)} %bitcast.4), custom_call_target="tpu_custom_call" | custom-call | tf_op jit(solution)/shard_map/pallas_call | solution.py:271
  67.0 1.9 %copy.7 = bf16[1,1024,256]{2,1,0:T(8,128)(2,1)} copy(bf16[1,1024,256]{2,1,0:T(8,128)(2,1)} %bitcast.3) | data formatting | bytes 1048576

commit v3 on v2

--- a/solution.py
+++ b/solution.py
@@ -91,32 +91,27 @@
     for q in range(nk):
         fields_out[q] = fields_ref[q : q + 1, :]
     fields_in[me] = fields_out[me]
-    pl.semaphore_wait(barrier, n - 1)
-
-    def field_copy(peer, slot, r):
-        return pltpu.make_async_remote_copy(
-            src_ref=fields_out.at[peer], dst_ref=fields_in.at[slot], send_sem=fsend.at[r],
-            recv_sem=frecv.at[slot], device_id={"pb": peer}, device_id_type=MESH,
-        )
-
-    for r in places:
-        field_copy(peer_of(r), me, r).start()
-
     spread[...] = (
         lax.broadcasted_iota(jnp.int32, (group, wide), 1) // ROWS
         == lax.broadcasted_iota(jnp.int32, (group, wide), 0)
     ).astype(jnp.float32).astype(jnp.bfloat16)
-    square = lax.broadcasted_iota(jnp.int32, (norb, norb), 0) == lax.broadcasted_iota(
-        jnp.int32, (norb, norb), 1
-    )
-    for k in range(nk):
-        row = jnp.broadcast_to(onebody_ref[k : k + 1, :], (norb, norb))
-        column = jnp.sum(jnp.where(square, row, 0.0), axis=1, keepdims=True)
-        diag[k * norb : (k + 1) * norb, :] = jnp.broadcast_to(column, (norb, 128))
+    pl.semaphore_wait(barrier, n - 1)
+
+    def field_copy(peer, slot, r):
+        return pltpu.make_async_remote_copy(
+            src_ref=fields_out.at[peer], dst_ref=fields_in.at[slot], send_sem=fsend,
+            recv_sem=frecv, device_id={"pb": peer}, device_id_type=MESH,
+        )
 
     for r in places:
-        peer = peer_of(r)
-        field_copy(peer, peer, r).wait_recv()
+        field_copy(peer_of(r), me, r).start()
+
+    others = pl.ds(0, n - 1)
+    all_fields = pltpu.make_async_remote_copy(
+        src_ref=fields_out.at[others], dst_ref=fields_in.at[others], send_sem=fsend,
+        recv_sem=frecv, device_id={"pb": peer_of(0)}, device_id_type=MESH,
+    )
+    all_fields.wait_recv()
     for r in range(n):
         lines[r : r + 1, :] = fields_in[peer_of(r)]
 
@@ -128,8 +123,8 @@
 
     def block_copy(c, peer, slot, r):
         return pltpu.make_async_remote_copy(
-            src_ref=blocks_out.at[c, r], dst_ref=blocks_in.at[c, slot], send_sem=bsend.at[c, r],
-            recv_sem=brecv.at[c, slot], device_id={"pb": peer}, device_id_type=MESH,
+            src_ref=blocks_out.at[c, r], dst_ref=blocks_in.at[c, slot], send_sem=bsend,
+            recv_sem=brecv.at[c], device_id={"pb": peer}, device_id_type=MESH,
         )
 
     vectors_piece = PIECE // ROWS
@@ -198,6 +193,14 @@
         return carry
 
     lax.fori_loop(0, chunks, compute, 0)
+    square = lax.broadcasted_iota(jnp.int32, (norb, norb), 0) == lax.broadcasted_iota(
+        jnp.int32, (norb, norb), 1
+    )
+    for k in range(nk):
+        row = jnp.broadcast_to(onebody_ref[k : k + 1, :], (norb, norb))
+        column = jnp.sum(jnp.where(square, row, 0.0), axis=1, keepdims=True)
+        diag[k * norb : (k + 1) * norb, :] = jnp.broadcast_to(column, (norb, 128))
+
     walker_copy.wait()
 
     def finish(product, here, weight, number):
@@ -206,9 +209,10 @@
 
     def assemble(c, carry):
         i, h = c // SPLITS, c % SPLITS
-        for r in places:
-            peer = peer_of(r)
-            block_copy(c, peer, peer, r).wait_recv()
+        pltpu.make_async_remote_copy(
+            src_ref=blocks_out.at[c, others], dst_ref=blocks_in.at[c, others], send_sem=bsend,
+            recv_sem=brecv.at[c], device_id={"pb": peer_of(0)}, device_id_type=MESH,
+        ).wait_recv()
         for kk in range(k_here):
             k = h * k_here + kk
             lane = kk // 2 * 128
@@ -246,15 +250,11 @@
             else:
                 out_ref[rows, :] = after.astype(jnp.bfloat16)
 
-    for r in places:
-        field_copy(peer_of(r), me, r).wait_send()
-
-    def drain(c, carry):
-        for r in places:
-            block_copy(c, peer_of(r), me, r).wait_send()
-        return carry
-
-    lax.fori_loop(0, chunks, drain, 0)
+    all_fields.wait_send()
+    pltpu.make_async_remote_copy(
+        src_ref=blocks_out.at[:, others], dst_ref=blocks_in.at[:, others], send_sem=bsend,
+        recv_sem=brecv.at[0], device_id={"pb": peer_of(0)}, device_id_type=MESH,
+    ).wait_send()
 
 
 def fused(fields, field_shift, cholesky, onebody, walkers):
@@ -290,11 +290,11 @@
             pltpu.VMEM((size, columns), bf16),
             pltpu.VMEM((size, columns), bf16),
             pltpu.VMEM((size, columns), bf16),
-            pltpu.SemaphoreType.DMA((n,)),
-            pltpu.SemaphoreType.DMA((n,)),
+            pltpu.SemaphoreType.DMA,
+            pltpu.SemaphoreType.DMA,
             pltpu.SemaphoreType.DMA((SLOTS,)),
-            pltpu.SemaphoreType.DMA((chunks, n)),
-            pltpu.SemaphoreType.DMA((chunks, n)),
+            pltpu.SemaphoreType.DMA,
+            pltpu.SemaphoreType.DMA((chunks,)),
             pltpu.SemaphoreType.DMA,
         ],
         compiler_params=pltpu.CompilerParams(

time: 69.1 us -> 66.4 us (0.961)
  Pallas kernels: 67 us -> 64.3 us
    pallas_call x1, Pallas kernels: 67 us -> 64.3 us  [fused(): pl.pallas_call(functools.partial(kernel, n, nk, norb), out_shape=jax.Shap...]
where the time goes in v3:
time: 66.4 us; the launch traced here: 66.2 us
  Pallas kernels  64.3 us (97%)
  local copies, waits for them, and re-layouts  1.87 us (3%)
    pallas_call x1, Pallas kernels, fused(): pl.pallas_call(functools.partial(kernel, n, nk, norb), out_shape=jax.Shap...  64.3 us
    unnamed x1, local copies, waits for them, and re-layouts  1.87 us

profile of v3, /device:TPU:0, one launch (start us, length us, event | category | flops | bytes accessed | tf_op | source)
XLA Modules:
  0.0 66.2 jit_solution(7451341838445369489)
XLA Ops:
  0.0 64.3 %shard_map.55 = bf16[1024,256]{1,0:T(8,128)(2,1)} custom-call(f32[16,512]{1,0:T(8,128)} %bitcast.5, f32[16,512]{1,0:T(8,128)} %shift_ref.1, f32[16,64]{1,0:T(8,128)} %onebody_ref.1, bf16[512,64,1024]{2,1,0:T(8,128)(2,1)} %chol_ref.1, bf16[1024,256]{1,0:T(8,128)(2,1)} %bitcast.4), custom_call_target="tpu_custom_call" | custom-call | tf_op jit(solution)/shard_map/pallas_call | solution.py:271
  64.3 1.9 %copy.7 = bf16[1,1024,256]{2,1,0:T(8,128)(2,1)} copy(bf16[1,1024,256]{2,1,0:T(8,128)(2,1)} %bitcast.3) | data formatting | bytes 1048576
